TPU v7x, 32 devices: a whole 2x2x4 slice. The times are simulated.
32 devices in a mesh: dp: 4 (over x, core), group: 8 (over z, y).
Axes of the slice: x: 2, y: 2, z: 4, core: 2. Of those that a mesh axis runs over, the one named last changes fastest.
Arguments:
- features: bfloat16 [8192, 3072], P(('dp', 'group')), may hold values from -6 to 6
- target_embed: bfloat16 [8192, 256], P(('dp', 'group')), may hold values from -80 to 80
- proj_weight: bfloat16 [3072, 256], replicated, may hold values from -0.109375 to 0.109375
- prototypes: float32 [2048, 256], replicated, may hold values from -20 to 20
Outputs:
- grad_feat: bfloat16 [8192, 3072], P(('dp', 'group'))
- grad_proj: float32 [3072, 256], P('group')
- grad_protos: float32 [2048, 256], replicated
All inputs are finite; a program needn't handle non-finite values.
Results may differ from a plain program's by a relative error of at most 0.0067.
Values sent between devices are 32-bit elements; how exact they have to be, the bound alone decides.
A program may use at most 64 MiB of HBM per device.

v0:
```python
import jax
import jax.numpy as jnp
from jax import lax
from jax.sharding import PartitionSpec as P

SWEEPS = 3


def normalize(values):
    return values * lax.rsqrt(jnp.sum(values * values, axis=-1, keepdims=True) + 1e-06)


def rownorm(matrix):
    return matrix / jnp.sum(matrix, axis=1, keepdims=True)


def column_total(partial_value):
    return lax.psum(partial_value, ("dp", "group"))


def local(features, target_embed, proj_weight, prototypes):
    unit_protos, proto_back = jax.vjp(normalize, prototypes)
    proto_b = unit_protos.astype(jnp.bfloat16)
    target_b = normalize(target_embed.astype(jnp.float32)).astype(jnp.bfloat16)
    scores = jnp.dot(target_b, proto_b.T, preferred_element_type=jnp.float32)
    plan = rownorm(jnp.exp(scores * (1.0 / 0.05)))
    for sweep in range(SWEEPS):
        colsum = column_total(jnp.sum(plan, axis=0))
        plan = rownorm(plan / colsum)
    hidden = jnp.dot(features, proj_weight, preferred_element_type=jnp.float32)
    embed, embed_back = jax.vjp(normalize, hidden)
    embed_b = embed.astype(jnp.bfloat16)
    online = jnp.dot(embed_b, proto_b.T, preferred_element_type=jnp.float32)
    prob = jax.nn.softmax(online * (1.0 / 0.1), axis=1)
    grad_scores = ((prob - plan) * (1.0 / 0.1)).astype(jnp.bfloat16)
    local_unit = lax.dot_general(
        grad_scores, embed_b, (((0,), (0,)), ((), ())), preferred_element_type=jnp.float32
    )
    grad_unit = lax.psum(local_unit, ("dp", "group"))
    grad_protos = proto_back(grad_unit)[0]
    grad_embed = jnp.dot(grad_scores, proto_b, preferred_element_type=jnp.float32)
    grad_hidden = embed_back(grad_embed)[0].astype(jnp.bfloat16)
    grad_feat = lax.dot_general(
        grad_hidden, proj_weight, (((1,), (1,)), ((), ())), preferred_element_type=jnp.float32
    ).astype(jnp.bfloat16)
    grad_part = lax.psum_scatter(
        lax.dot_general(
            features, grad_hidden, (((0,), (0,)), ((), ())), preferred_element_type=jnp.float32
        ),
        "group",
        scatter_dimension=0,
        tiled=True,
    )
    grad_proj = lax.psum(grad_part, "dp")
    return (grad_feat, grad_proj, grad_protos)


def solution(mesh):
    return jax.shard_map(
        local,
        mesh=mesh,
        in_specs=(P(("dp", "group"), None), P(("dp", "group"), None), P(), P()),
        out_specs=(P(("dp", "group"), None), P("group", None), P()),
        check_vma=False,
    )
```

profile of v0, /device:TPU:0, one launch (start us, length us, event | category | flops | bytes accessed | tf_op | source)
XLA Modules:
  0.0 346.1 jit_solution(14579434763321458965)
XLA Ops:
  8.1 2.1 multiply_reduce_fusion.1
  11.3 0.6 fusion.23
  11.8 1.3 copy-done.1
  13.5 42.1 %psum.35 = f32[2048]{0:T(1024)S(1)} all-reduce(f32[2048]{0:T(1024)S(1)} %divide_reduce_fusion), channel_id=1, replica_groups=mesh['dp'=4,'group'=8] {'dp','group'}, use_global_device_ids=true, to_apply=%region_7.0 | all-reduce | flops 2048 | bytes 16384 | tf_op jit(solution)/shard_map/psum | solution.py:18
  55.6 2.2 fusion.11
  58.2 40.2 %psum.36 = f32[2048]{0:T(1024)S(1)} all-reduce(f32[2048]{0:T(1024)S(1)} %fusion.12), channel_id=1, replica_groups=mesh['dp'=4,'group'=8] {'dp','group'}, use_global_device_ids=true, to_apply=%region_10.0 | all-reduce | flops 2048 | bytes 16384 | tf_op jit(solution)/shard_map/psum | solution.py:18
  98.5 2.3 fusion.13
  100.8 0.7 fusion.14
  101.4 40.1 %psum.37 = f32[2048]{0:T(1024)S(1)} all-reduce(f32[2048]{0:T(1024)S(1)} %fusion.14), channel_id=1, replica_groups=mesh['dp'=4,'group'=8] {'dp','group'}, use_global_device_ids=true, to_apply=%region_13.0 | all-reduce | flops 2048 | bytes 16384 | tf_op jit(solution)/shard_map/psum | solution.py:18
  141.5 2.4 fusion.15
  144.0 0.8 multiply_reduce_fusion.3
  145.8 0.6 copy-done.4
  146.4 1.4 multiply_convert_fusion
  147.8 1.0 copy-done.6
  148.7 1.8 fusion.22
  150.6 1.8 multiply_reduce_fusion.2
  152.4 2.2 convolution_bitcast_fusion
  154.8 1.4 copy-done.8
  156.2 1.8 convolution_convert_fusion
  158.0 144.7 %all-reduce.5.cloned.1.call-done = f32[2048,256]{1,0:T(8,128)} async-done(((f32[2048,256]{1,0:T(8,128)}), f32[2048,256]{1,0:T(8,128)}) %all-reduce.5.cloned.1.call-update) | async-done | bytes 2097168 | tf_op jit(solution)/shard_map/psum | solution.py:39
  302.6 2.6 multiply_reduce_fusion
  305.3 3.5 %add_add_fusion = f32[2048,256]{1,0:T(8,128)} fusion(f32[2048,256]{1,0:T(8,128)} %param.7, f32[2048,256]{1,0:T(8,128)} %all-reduce.5.cloned.1.call-done, f32[2048]{0:T(1024)S(1)} %multiply_multiply_fusion.1, f32[2048]{0:T(1024)S(1)} %add_rsqrt_fusion), kind=kLoop, calls=%fused_computation.2 | loop fusion | flops 2097152 | bytes 6307840 | tf_op jit(solution)/shard_map/transpose(jvp())/add_any | solution.py:10
  308.8 28.0 %all-reduce.3.cloned.1.call-done = f32[384,256]{0,1:T(8,128)} async-done(((f32[384,256]{0,1:T(8,128)}), f32[384,256]{0,1:T(8,128)}) %all-reduce.3.cloned.1.call-update) | async-done | bytes 393232 | tf_op jit(solution)/shard_map/psum | solution.py:54
  336.7 1.9 copy.7
  (35 shorter events, 3.2 us)
Async XLA Ops:
  8.0 136.0 %copy-start = (bf16[256,3072]{1,0:T(8,128)(2,1)S(1)}, bf16[256,3072]{1,0:T(8,128)(2,1)}, u32[]{:S(2)}) copy-start(bf16[256,3072]{1,0:T(8,128)(2,1)} %param.4) | copy-start | bytes 4718596
  8.0 294.6 %all-reduce.5.cloned.1.call-start = ((), (), s32[]{:S(2)}) async-start(), calls=%async_computation.3 | async-start | bytes 4194304 | tf_op jit(solution)/shard_map/psum | solution.py:39
  8.1 2.3 copy-start.5
  10.2 1.0 copy-start.9
  11.8 1.3 copy-start.1
  55.6 2.2 copy-start.2
  98.5 2.3 copy-start.3
  141.5 2.4 copy-start.7
  144.8 1.6 copy-start.4
  147.7 1.0 copy-start.6
  150.6 154.7 %reduce-scatter.2.cloned.1.call-start = ((), (), s32[]{:S(2)}) async-start(), calls=%async_computation.1 | async-start | bytes 3538944 | tf_op jit(solution)/shard_map/reduce_scatter | solution.py:46
  154.7 1.5 copy-start.8
  154.7 182.0 %all-reduce.3.cloned.1.call-start = ((), (), s32[]{:S(2)}) async-start(), calls=%async_computation.2 | async-start | bytes 786432 | tf_op jit(solution)/shard_map/psum | solution.py:54
Sparse Core Ops, SparseCore 0:
  150.7 151.9 all-reduce.4
Sparse Core Ops, SparseCore 1:
  154.8 82.1 reduce-scatter.1
  305.4 31.3 all-reduce.2
where the time goes:
time: 347 us; the launch traced here: 346 us
  waiting for transfers between devices  173 us (50%)
  blocking collectives  122 us (35%)
  other arithmetic  18.8 us (5%)
  between operations  15.7 us (5%)
  matrix products  9.52 us (3%)
  local copies, waits for them, and re-layouts  6.88 us (2%)
    psum x1, waiting for transfers between devices, local(): grad_unit = lax.psum(local_unit, ('dp', 'group'))  145 us
    psum x3, blocking collectives, column_total(): return lax.psum(partial_value, ('dp', 'group'))  122 us
    psum x1, waiting for transfers between devices, local(): grad_proj = lax.psum(grad_part, 'dp')  28 us
  transfers between devices with their start and end apart: 3, of which 2 were waited for; matrix products, arithmetic and copies ran while one was open for 3% of the time, Pallas kernels for 0%

commit v1 on v0

v1 whole, which is shorter than its diff:
```python
import functools

import jax
import jax.numpy as jnp
from jax import lax
from jax.experimental import pallas as pl
from jax.experimental.pallas import tpu as pltpu
from jax.sharding import PartitionSpec as P

SWEEPS = 3
MESH = pl.DeviceIdType.MESH
F32 = jnp.float32
BF16 = jnp.bfloat16


def normalize(values):
    return values * lax.rsqrt(jnp.sum(values * values, axis=-1, keepdims=True) + 1e-06)


def inv_norm(values):
    return lax.rsqrt(jnp.sum(values * values, axis=-1, keepdims=True) + 1e-06)


def dot(a, b, ca, cb):
    return lax.dot_general(a, b, (((ca,), (cb,)), ((), ())), preferred_element_type=F32)


def others(n, body):
    if n <= 8:
        for k in range(1, n):
            body(k)
    else:
        lax.fori_loop(1, n, lambda k, c: (body(k), c)[1], 0)


def peer_of(me, k, n):
    return lax.rem(me + k, n)


def scores_kernel(
    n_dp, n_group, feat, target, proj, protos, gs_out, embed_out, gh_out,
    kern, proto_b, slots_d, slots_g, w, hid, send_d, recv_d, send_g, recv_g,
):
    d = lax.axis_index("dp")
    g = lax.axis_index("group")
    barrier = pltpu.get_barrier_semaphore()
    others(n_dp, lambda k: pl.semaphore_signal(
        barrier, inc=1, device_id=(peer_of(d, k, n_dp), g), device_id_type=MESH))
    others(n_group, lambda k: pl.semaphore_signal(
        barrier, inc=1, device_id=(d, peer_of(g, k, n_group)), device_id_type=MESH))

    def copy_d(s, k, owner, peer):
        return pltpu.make_async_remote_copy(
            src_ref=slots_d.at[s, owner], dst_ref=slots_d.at[s, owner],
            send_sem=send_d.at[s, k], recv_sem=recv_d.at[s, owner],
            device_id=(peer, g), device_id_type=MESH)

    def copy_g(s, k, owner, peer):
        return pltpu.make_async_remote_copy(
            src_ref=slots_g.at[s, owner], dst_ref=slots_g.at[s, owner],
            send_sem=send_g.at[s, k], recv_sem=recv_g.at[s, owner],
            device_id=(d, peer), device_id_type=MESH)

    proto_b[...] = normalize(protos[...]).astype(BF16)
    target_b = normalize(target[...].astype(F32)).astype(BF16)
    kern[...] = jnp.exp(dot(target_b, proto_b[...], 1, 1) * (1.0 / 0.05))
    w[...] = jnp.ones_like(w)
    for s in range(SWEEPS):
        row = jnp.sum(kern[...] * w[...], axis=1, keepdims=True)
        slots_d[s, d] = jnp.sum(kern[...] * (1.0 / row), axis=0, keepdims=True)
        if s == 0:
            pl.semaphore_wait(barrier, n_dp - 1 + n_group - 1)
        others(n_dp, lambda k: copy_d(s, k, d, peer_of(d, k, n_dp)).start())
        if s == 0:
            hid[...] = dot(feat[...], proj[...], 1, 0)
        others(n_dp, lambda k: copy_d(s, k, peer_of(d, k, n_dp), d).wait_recv())
        slots_g[s, g] = jnp.sum(slots_d[s], axis=0)
        others(n_group, lambda k: copy_g(s, k, g, peer_of(g, k, n_group)).start())
        if s == 0:
            embed_out[...] = (hid[...] * inv_norm(hid[...])).astype(BF16)
        others(n_group, lambda k: copy_g(s, k, peer_of(g, k, n_group), g).wait_recv())
        w[...] = 1.0 / jnp.sum(slots_g[s], axis=0)
    plan = kern[...] * w[...]
    plan = plan / jnp.sum(plan, axis=1, keepdims=True)
    prob = jnp.exp(dot(embed_out[...], proto_b[...], 1, 1) * (1.0 / 0.1))
    prob = prob / jnp.sum(prob, axis=1, keepdims=True)
    gs_out[...] = ((prob - plan) * (1.0 / 0.1)).astype(BF16)
    ge = dot(gs_out[...], proto_b[...], 1, 0)
    scale = inv_norm(hid[...])
    embed = hid[...] * scale
    gh = scale * (ge - embed * jnp.sum(embed * ge, axis=-1, keepdims=True))
    gh_out[...] = gh.astype(BF16)
    for s in range(SWEEPS):
        others(n_dp, lambda k: copy_d(s, k, d, peer_of(d, k, n_dp)).wait_send())
        others(n_group, lambda k: copy_g(s, k, g, peer_of(g, k, n_group)).wait_send())


def scores(n_dp, n_group, features, target_embed, proj_weight, prototypes):
    rows = features.shape[0]
    count, width = prototypes.shape
    vmem = pl.BlockSpec(memory_space=pltpu.VMEM)
    return pl.pallas_call(
        functools.partial(scores_kernel, n_dp, n_group),
        out_shape=(
            jax.ShapeDtypeStruct((rows, count), BF16),
            jax.ShapeDtypeStruct((rows, width), BF16),
            jax.ShapeDtypeStruct((rows, width), BF16),
        ),
        in_specs=[vmem] * 4,
        out_specs=(vmem,) * 3,
        scratch_shapes=[
            pltpu.VMEM((rows, count), F32),
            pltpu.VMEM((count, width), BF16),
            pltpu.VMEM((SWEEPS, n_dp, 1, count), F32),
            pltpu.VMEM((SWEEPS, n_group, 1, count), F32),
            pltpu.VMEM((1, count), F32),
            pltpu.VMEM((rows, width), F32),
            pltpu.SemaphoreType.DMA((SWEEPS, n_dp)),
            pltpu.SemaphoreType.DMA((SWEEPS, n_dp)),
            pltpu.SemaphoreType.DMA((SWEEPS, n_group)),
            pltpu.SemaphoreType.DMA((SWEEPS, n_group)),
        ],
        compiler_params=pltpu.CompilerParams(
            collective_id=0, has_side_effects=True, vmem_limit_bytes=48 << 20),
        name="scores",
    )(features, target_embed, proj_weight, prototypes)


def sums_kernel(
    n_dp, n_group, gs, embed, feat, gh, proj, unit, pout, gfeat,
    ub, uc, ux, uy, uz, pb, pc, py, pz, px, sem_s, sem_r,
):
    nx, nz = n_dp // 2, n_group // 2
    dp = lax.axis_index("dp")
    grp = lax.axis_index("group")
    x, c = dp // 2, lax.rem(dp, 2)
    z, y = grp // 2, lax.rem(grp, 2)
    count, feats = gs.shape[1], feat.shape[1]

    def at_c(i):
        return (x * 2 + i, grp)

    def at_x(i):
        return (i * 2 + c, grp)

    def at_y(i):
        return (dp, z * 2 + i)

    def at_z(i):
        return (dp, i * 2 + y)

    axes = {"c": (at_c, c, 2), "x": (at_x, x, nx), "y": (at_y, y, 2), "z": (at_z, z, nz)}
    barrier = pltpu.get_barrier_semaphore()
    total = 0
    for at, me, n in axes.values():
        total += n - 1
        for k in range(1, n):
            pl.semaphore_signal(
                barrier, inc=1, device_id=at(peer_of(me, k, n)), device_id_type=MESH)

    base = {}
    sends = []

    def stage(name, axis, src_of, dst_of):
        at, me, n = axes[axis]
        first = base.setdefault(name, sum(v for _, v in used))
        used.append((name, n))

        def make(k, to, sender, peer):
            return pltpu.make_async_remote_copy(
                src_ref=src_of(to), dst_ref=dst_of(sender),
                send_sem=sem_s.at[first + k], recv_sem=sem_r.at[first + sender],
                device_id=at(peer), device_id_type=MESH)

        out = [make(k, peer_of(me, k, n), me, peer_of(me, k, n)) for k in range(1, n)]
        for copy in out:
            copy.start()
        sends.extend(out)

        def wait():
            for k in range(1, n):
                other = peer_of(me, k, n)
                make(k, me, other, other).wait_recv()
        return wait

    used = []

    def land(buf, axis):
        n = axes[axis][2]
        return lambda j: buf.at[j]

    def rows(ref, index, size):
        return ref.at[pl.ds(pl.multiple_of(index * size, size), size)]

    half = count // 2
    r_x, r_y, r_z = half // nx, half // nx // 2, half // nx // 2 // nz

    def unit_half(i):
        cols = pl.ds(pl.multiple_of(i * half, half), half)
        ub[i] = dot(gs[:, cols], embed[...], 0, 0)

    unit_half(1 - c)
    pl.semaphore_wait(barrier, total)
    w_uc = stage("uc", "c", lambda i: ub.at[i], lambda j: uc)
    unit_half(c)

    block = feats // n_group
    hb = block // 2
    hx = hb // nx
    for i in range(n_group):
        part = dot(feat[:, i * block:(i + 1) * block], gh[...], 0, 0)
        for j in range(2):
            pb[j, i % 2, i // 2] = part[j * hb:(j + 1) * hb]
    w_pc = stage("pc", "c", lambda i: pb.at[i], lambda j: pc)

    w_uc()
    ub[c] += uc[...]
    mine = ub.at[c]
    w_ux = stage("ux", "x", lambda i: rows(mine, i, r_x), lambda j: ux.at[j])
    w_pc()
    pb[c] += pc[...]
    w_py = stage("py", "y", lambda i: pb.at[c, i], lambda j: py)
    gfeat[...] = dot(gh[...], proj[...], 1, 1).astype(BF16)

    def add_all(dst, buf, axis):
        _, me, n = axes[axis]
        value = dst[...]
        for k in range(1, n):
            value = value + buf[peer_of(me, k, n)]
        dst[...] = value

    w_ux()
    ux_me = rows(mine, x, r_x)
    add_all(ux_me, ux, "x")
    w_uy = stage("uy", "y", lambda i: rows(ux_me, i, r_y), lambda j: uy)
    w_py()
    pb[c, y] += py[...]
    w_pz = stage("pz", "z", lambda i: pb.at[c, y, i], lambda j: pz.at[j])
    w_uy()
    uy_me = rows(ux_me, y, r_y)
    uy_me[...] += uy[...]
    w_uz = stage("uz", "z", lambda i: rows(uy_me, i, r_z), lambda j: uz.at[j])
    w_uz()
    def out_c(i):
        return rows(unit, i, half)

    def out_x(i):
        return rows(out_c(c), i, r_x)

    def out_y(i):
        return rows(out_x(x), i, r_y)

    def out_z(i):
        return rows(out_y(y), i, r_z)

    value = rows(uy_me, z, r_z)[...]
    for k in range(1, nz):
        value = value + uz[peer_of(z, k, nz)]
    out_z(z)[...] = value
    g_uz = stage("gz", "z", lambda i: out_z(z), lambda j: out_z(j))
    g_uz()
    g_uy = stage("gy", "y", lambda i: out_y(y), lambda j: out_y(j))
    w_pz()
    pz_me = pb.at[c, y, z]
    add_all(pz_me, pz, "z")
    w_px = stage("px", "x", lambda i: rows(pz_me, i, hx), lambda j: px.at[j])
    g_uy()
    g_ux = stage("gx", "x", lambda i: out_x(x), lambda j: out_x(j))
    w_px()

    def pout_c(i):
        return rows(pout, i, hb)

    def pout_x(i):
        return rows(pout_c(c), i, hx)

    value = rows(pz_me, x, hx)[...]
    for k in range(1, nx):
        value = value + px[peer_of(x, k, nx)]
    pout_x(x)[...] = value
    g_px = stage("hx", "x", lambda i: pout_x(x), lambda j: pout_x(j))
    g_ux()
    g_uc = stage("gc", "c", lambda i: out_c(c), lambda j: out_c(j))
    g_px()
    g_pc = stage("hc", "c", lambda i: pout_c(c), lambda j: pout_c(j))
    g_uc()
    g_pc()
    for copy in sends:
        copy.wait_send()


def sums(n_dp, n_group, grad_scores, embed_b, features, grad_hidden, proj_weight):
    nx, nz = n_dp // 2, n_group // 2
    count, feats, width = grad_scores.shape[1], features.shape[1], embed_b.shape[1]
    half = count // 2
    r_x = half // nx
    r_y = r_x // 2
    r_z = r_y // nz
    hb = feats // n_group // 2
    hx = hb // nx
    vmem = pl.BlockSpec(memory_space=pltpu.VMEM)
    n_sem = 16 * max(2, nx, nz)
    return pl.pallas_call(
        functools.partial(sums_kernel, n_dp, n_group),
        out_shape=(
            jax.ShapeDtypeStruct((count, width), F32),
            jax.ShapeDtypeStruct((feats // n_group, width), F32),
            jax.ShapeDtypeStruct(features.shape, BF16),
        ),
        in_specs=[vmem] * 5,
        out_specs=(vmem,) * 3,
        scratch_shapes=[
            pltpu.VMEM((2, half, width), F32),
            pltpu.VMEM((half, width), F32),
            pltpu.VMEM((nx, r_x, width), F32),
            pltpu.VMEM((r_y, width), F32),
            pltpu.VMEM((nz, r_z, width), F32),
            pltpu.VMEM((2, 2, nz, hb, width), F32),
            pltpu.VMEM((2, nz, hb, width), F32),
            pltpu.VMEM((nz, hb, width), F32),
            pltpu.VMEM((nz, hb, width), F32),
            pltpu.VMEM((nx, hx, width), F32),
            pltpu.SemaphoreType.DMA((n_sem,)),
            pltpu.SemaphoreType.DMA((n_sem,)),
        ],
        compiler_params=pltpu.CompilerParams(
            collective_id=1, has_side_effects=True, vmem_limit_bytes=48 << 20),
        name="sums",
    )(grad_scores, embed_b, features, grad_hidden, proj_weight)


def plain_sums(grad_scores, embed_b, features, grad_hidden, proj_weight):
    grad_unit = lax.psum(dot(grad_scores, embed_b, 0, 0), ("dp", "group"))
    grad_feat = dot(grad_hidden, proj_weight, 1, 1).astype(BF16)
    part = lax.psum_scatter(
        dot(features, grad_hidden, 0, 0), "group", scatter_dimension=0, tiled=True)
    return grad_unit, lax.psum(part, "dp"), grad_feat


def solution(mesh):
    n_dp, n_group = mesh.shape["dp"], mesh.shape["group"]

    def local(features, target_embed, proj_weight, prototypes):
        grad_scores, embed_b, grad_hidden = scores(
            n_dp, n_group, features, target_embed, proj_weight, prototypes)
        args = (grad_scores, embed_b, features, grad_hidden, proj_weight)
        unit = 8 * n_dp * n_group
        even = n_dp % 2 == 0 and n_group % 2 == 0
        if even and prototypes.shape[0] % unit == 0 and features.shape[1] % unit == 0:
            grad_unit, grad_proj, grad_feat = sums(n_dp, n_group, *args)
        else:
            grad_unit, grad_proj, grad_feat = plain_sums(*args)
        scale = inv_norm(prototypes)
        unit_protos = prototypes * scale
        along = jnp.sum(unit_protos * grad_unit, axis=-1, keepdims=True)
        grad_protos = (grad_unit - unit_protos * along) * scale
        return (grad_feat, grad_proj, grad_protos)

    return jax.shard_map(
        local,
        mesh=mesh,
        in_specs=(P(("dp", "group"), None), P(("dp", "group"), None), P(), P()),
        out_specs=(P(("dp", "group"), None), P("group", None), P()),
        check_vma=False,
    )
```

time: 347 us -> 123 us (0.35)
  waiting for transfers between devices: 173 us -> 0 us
  blocking collectives: 122 us -> 0 us
  Pallas kernels: 0 us -> 113 us
  between operations: 15.7 us -> 0.74 us
  other arithmetic: 18.8 us -> 6.12 us
  matrix products: 9.52 us -> 0 us
  local copies, waits for them, and re-layouts: 6.88 us -> 3.31 us
    psum x2 -> x0, waiting for transfers between devices: 173 us -> none  [the longest x1 145 us: local(): grad_unit = lax.psum(local_unit, ('dp', 'group'))]
    psum x3 -> x0, blocking collectives: 122 us -> none  [column_total(): return lax.psum(partial_value, ('dp', 'group'))]
    pallas_call x0 -> x2, Pallas kernels: none -> 113 us  [the longest x1 81.8 us: sums(): pl.pallas_call(functools.partial(sums_kernel, n_dp, n_group), out_shape=(...]
    dot_general x7 -> x0, matrix products: 9.52 us -> none  [the longest x1 2.25 us: local(): lax.dot_general(features, grad_hidden, (((0,), (0,)), ((), ())), preferre...]
    reduce_sum x10 -> x2, other arithmetic: 13.5 us -> 4.43 us  [the longest x1 2.37 us: local(): along = jnp.sum(unit_protos * grad_unit, axis=-1, keepdims=True)]
    unnamed x21 -> x12, local copies, waits for them, and re-layouts: 6.88 us -> 3.31 us
    add_any x1 -> x0, other arithmetic: 3.5 us -> none  [normalize(): values * values]
  transfers between devices with their start and end apart: 3 -> 0, of which waited for: 2 -> 0; matrix products, arithmetic and copies ran while one was open for 3% -> 0% of each run, Pallas kernels for 0% -> 0%
where the time goes in v1:
time: 123 us
  Pallas kernels  113 us (92%)
  other arithmetic  6.12 us (5%)
  local copies, waits for them, and re-layouts  3.31 us (3%)
    pallas_call x1, Pallas kernels, sums(): pl.pallas_call(functools.partial(sums_kernel, n_dp, n_group), out_shape=(...  81.8 us
    pallas_call x1, Pallas kernels, scores(): pl.pallas_call(functools.partial(scores_kernel, n_dp, n_group), out_shape...  30.8 us
    unnamed x12, local copies, waits for them, and re-layouts  3.31 us

profile of v1, /device:TPU:0, one launch (start us, length us, event | category | flops | bytes accessed | tf_op | source)
XLA Modules:
  0.0 122.8 jit_solution(3342908501684349843)
XLA Ops:
  0.6 0.0 copy-start
  0.6 0.0 copy-start.2
  0.6 2.1 %multiply_reduce_fusion.1 = f32[2048]{0:T(1024)S(1)} fusion(f32[2048,256]{1,0:T(8,128)} %protos.1), kind=kLoop, calls=%fused_computation.2 | loop fusion | flops 1046528 | bytes 2105344 | tf_op jit(solution)/shard_map/reduce_sum | solution.py:21
  2.7 0.0 copy-done
  2.7 0.0 copy-done.2
  2.7 0.0 copy-start.1
  2.8 1.4 %copy-done.1 = bf16[3072,256]{1,0:T(8,128)(2,1)S(1)} copy-done((bf16[3072,256]{1,0:T(8,128)(2,1)S(1)}, bf16[3072,256]{1,0:T(8,128)(2,1)}, u32[]{:S(2)}) %copy-start.1) | copy-done | bytes 1572888
  4.2 30.8 %scores.1 = (bf16[256,2048]{1,0:T(8,128)(2,1)S(1)}, bf16[256,256]{1,0:T(8,128)(2,1)S(1)}, bf16[256,256]{1,0:T(8,128)(2,1)S(1)}) custom-call(bf16[256,3072]{1,0:T(8,128)(2,1)S(1)} %copy-done, bf16[256,256]{1,0:T(8,128)(2,1)S(1)} %copy-done.2, bf16[3072,256]{1,0:T(8,128)(2,1)S(1)} %copy-done.1, f32[2048,256]{1,0:T(8,128)} %protos.1), custom_call_target="tpu_custom_call" | custom-call | tf_op jit(solution)/shard_map/scores/pallas_call | solution.py:102
  35.0 0.0 copy-start.3
  35.0 81.8 %sums.1 = (f32[2048,256]{1,0:T(8,128)}, f32[384,256]{1,0:T(8,128)S(1)}, bf16[256,3072]{1,0:T(8,128)(2,1)S(1)}) custom-call(bf16[256,2048]{1,0:T(8,128)(2,1)S(1)} %get-tuple-element.9.gs, bf16[256,256]{1,0:T(8,128)(2,1)S(1)} %get-tuple-element.10.embed, bf16[256,3072]{1,0:T(8,128)(2,1)S(1)} %copy-done, bf16[256,256]{1,0:T(8,128)(2,1)S(1)} %get-tuple-element.11.gh, ...), custom_call_target="tpu_custom_call" | custom-call | tf_op jit(solution)/shard_map/sums/pallas_call | solution.py:303
  116.8 0.0 copy-done.3
  116.8 0.0 copy-start.4
  116.8 2.4 %multiply_reduce_fusion = f32[2048]{0:T(1024)S(1)} fusion(f32[2048,256]{1,0:T(8,128)} %get-tuple-element.14, f32[2048,256]{1,0:T(8,128)S(1)} %copy-done.3, f32[2048]{0:T(1024)S(1)} %add_rsqrt_fusion), kind=kLoop, calls=%fused_computation.1 | loop fusion | flops 1570816 | bytes 4210688 | tf_op jit(solution)/shard_map/reduce_sum | solution.py:355
  119.2 0.0 copy-done.4
  119.2 1.7 %subtract_multiply_fusion = f32[2048,256]{1,0:T(8,128)} fusion(f32[2048,256]{1,0:T(8,128)S(1)} %copy-done.4, f32[2048,256]{1,0:T(8,128)S(1)} %copy-done.3, f32[2048]{0:T(1024)S(1)} %multiply_reduce_fusion, f32[2048]{0:T(1024)S(1)} %add_rsqrt_fusion), kind=kLoop, calls=%fused_computation | loop fusion | flops 2097152 | bytes 6307840 | tf_op jit(solution)/shard_map/mul | solution.py:356
  120.9 1.1 copy.9
  122.0 0.7 copy.10
  (1 shorter events, 0.0 us)
Async XLA Ops:
  0.6 2.1 %copy-start = (bf16[256,3072]{1,0:T(8,128)(2,1)S(1)}, bf16[256,3072]{1,0:T(8,128)(2,1)}, u32[]{:S(2)}) copy-start(bf16[256,3072]{1,0:T(8,128)(2,1)} %feat.3) | copy-start | bytes 4718596
  0.6 2.1 %copy-start.2 = (bf16[256,256]{1,0:T(8,128)(2,1)S(1)}, bf16[256,256]{1,0:T(8,128)(2,1)}, u32[]{:S(2)}) copy-start(bf16[256,256]{1,0:T(8,128)(2,1)} %target.1) | copy-start | bytes 393220
  2.7 1.4 %copy-start.1 = (bf16[3072,256]{1,0:T(8,128)(2,1)S(1)}, bf16[3072,256]{1,0:T(8,128)(2,1)}, u32[]{:S(2)}) copy-start(bf16[3072,256]{1,0:T(8,128)(2,1)} %proj.3) | copy-start | bytes 4718596
  35.0 81.8 %copy-start.3 = (f32[2048,256]{1,0:T(8,128)S(1)}, f32[2048,256]{1,0:T(8,128)}, u32[]{:S(2)}) copy-start(f32[2048,256]{1,0:T(8,128)} %protos.1) | copy-start | bytes 6291460
  116.8 2.4 %copy-start.4 = (f32[2048,256]{1,0:T(8,128)S(1)}, f32[2048,256]{1,0:T(8,128)}, u32[]{:S(2)}) copy-start(f32[2048,256]{1,0:T(8,128)} %get-tuple-element.14) | copy-start | bytes 6291460

commit v2 on v1

--- a/solution.py
+++ b/solution.py
@@ -126,30 +126,25 @@
     )(features, target_embed, proj_weight, prototypes)
 
 
+UNIT_ORDERS = ("cxyz", "cyxz", "cxyz", "cyxz")
+PROJ_ORDERS = ("cyzx", "cxzy", "cyzx", "cxzy")
+
+
 def sums_kernel(
     n_dp, n_group, gs, embed, feat, gh, proj, unit, pout, gfeat,
-    ub, uc, ux, uy, uz, pb, pc, py, pz, px, sem_s, sem_r,
+    ub, pb, landing, sem_s, sem_r,
 ):
     nx, nz = n_dp // 2, n_group // 2
     dp = lax.axis_index("dp")
     grp = lax.axis_index("group")
     x, c = dp // 2, lax.rem(dp, 2)
     z, y = grp // 2, lax.rem(grp, 2)
-    count, feats = gs.shape[1], feat.shape[1]
-
-    def at_c(i):
-        return (x * 2 + i, grp)
-
-    def at_x(i):
-        return (i * 2 + c, grp)
-
-    def at_y(i):
-        return (dp, z * 2 + i)
-
-    def at_z(i):
-        return (dp, i * 2 + y)
-
-    axes = {"c": (at_c, c, 2), "x": (at_x, x, nx), "y": (at_y, y, 2), "z": (at_z, z, nz)}
+    axes = {
+        "c": (lambda i: (x * 2 + i, grp), c, 2),
+        "x": (lambda i: (i * 2 + c, grp), x, nx),
+        "y": (lambda i: (dp, z * 2 + i), y, 2),
+        "z": (lambda i: (dp, i * 2 + y), z, nz),
+    }
     barrier = pltpu.get_barrier_semaphore()
     total = 0
     for at, me, n in axes.values():
@@ -158,13 +153,17 @@
             pl.semaphore_signal(
                 barrier, inc=1, device_id=at(peer_of(me, k, n)), device_id_type=MESH)
 
-    base = {}
+    used = {"sem": 0, "row": 0}
     sends = []
 
-    def stage(name, axis, src_of, dst_of):
+    def take(what, amount):
+        first = used[what]
+        used[what] += amount
+        return first
+
+    def start(axis, src_of, dst_of):
         at, me, n = axes[axis]
-        first = base.setdefault(name, sum(v for _, v in used))
-        used.append((name, n))
+        first = take("sem", n)
 
         def make(k, to, sender, peer):
             return pltpu.make_async_remote_copy(
@@ -172,10 +171,10 @@
                 send_sem=sem_s.at[first + k], recv_sem=sem_r.at[first + sender],
                 device_id=at(peer), device_id_type=MESH)
 
-        out = [make(k, peer_of(me, k, n), me, peer_of(me, k, n)) for k in range(1, n)]
-        for copy in out:
+        for k in range(1, n):
+            copy = make(k, peer_of(me, k, n), me, peer_of(me, k, n))
             copy.start()
-        sends.extend(out)
+            sends.append(copy)
 
         def wait():
             for k in range(1, n):
@@ -183,123 +182,87 @@
                 make(k, me, other, other).wait_recv()
         return wait
 
-    used = []
-
-    def land(buf, axis):
-        n = axes[axis][2]
-        return lambda j: buf.at[j]
-
-    def rows(ref, index, size):
-        return ref.at[pl.ds(pl.multiple_of(index * size, size), size)]
-
-    half = count // 2
-    r_x, r_y, r_z = half // nx, half // nx // 2, half // nx // 2 // nz
-
-    def unit_half(i):
-        cols = pl.ds(pl.multiple_of(i * half, half), half)
-        ub[i] = dot(gs[:, cols], embed[...], 0, 0)
-
-    unit_half(1 - c)
+    def piece(ref, base, size):
+        return ref.at[pl.ds(pl.multiple_of(base, 8), size)]
+
+    def scatter(order, buf, base, size, out, out_base, gathered):
+        for step, axis in enumerate(order):
+            _, me, n = axes[axis]
+            size //= n
+            low, slots = base, take("row", n * size)
+            wait = start(
+                axis,
+                lambda i, low=low, size=size: piece(buf, low + i * size, size),
+                lambda j, slots=slots, size=size: piece(landing, slots + j * size, size))
+            yield
+            wait()
+            base = low + me * size
+            value = piece(buf, base, size)[...]
+            for k in range(1, n):
+                value = value + piece(landing, slots + peer_of(me, k, n) * size, size)[...]
+            last = step == len(order) - 1
+            piece(out if last else buf, out_base if last else base, size)[...] = value
+        base = out_base
+        for axis in gathered:
+            _, me, n = axes[axis]
+            low = base - me * size
+            wait = start(
+                axis,
+                lambda i, base=base, size=size: piece(out, base, size),
+                lambda j, low=low, size=size: piece(out, low + j * size, size))
+            yield
+            wait()
+            base, size = low, size * n
+
+    where = {"c": c, "x": x, "y": y, "z": z}
+    count, feats = gs.shape[1], feat.shape[1]
+    streams = []
+    size = count // len(UNIT_ORDERS)
+    ub[...] = dot(gs[...], embed[...], 0, 0)
     pl.semaphore_wait(barrier, total)
-    w_uc = stage("uc", "c", lambda i: ub.at[i], lambda j: uc)
-    unit_half(c)
+    for s, order in enumerate(UNIT_ORDERS):
+        own, part = s * size, size
+        for axis in order:
+            part //= axes[axis][2]
+            own = own + where[axis] * part
+        streams.append(scatter(order, ub, s * size, size, unit, own, order[::-1]))
+    for stream in streams:
+        next(stream)
 
     block = feats // n_group
-    hb = block // 2
-    hx = hb // nx
-    for i in range(n_group):
-        part = dot(feat[:, i * block:(i + 1) * block], gh[...], 0, 0)
-        for j in range(2):
-            pb[j, i % 2, i // 2] = part[j * hb:(j + 1) * hb]
-    w_pc = stage("pc", "c", lambda i: pb.at[i], lambda j: pc)
-
-    w_uc()
-    ub[c] += uc[...]
-    mine = ub.at[c]
-    w_ux = stage("ux", "x", lambda i: rows(mine, i, r_x), lambda j: ux.at[j])
-    w_pc()
-    pb[c] += pc[...]
-    w_py = stage("py", "y", lambda i: pb.at[c, i], lambda j: py)
-    gfeat[...] = dot(gh[...], proj[...], 1, 1).astype(BF16)
-
-    def add_all(dst, buf, axis):
-        _, me, n = axes[axis]
-        value = dst[...]
-        for k in range(1, n):
-            value = value + buf[peer_of(me, k, n)]
-        dst[...] = value
-
-    w_ux()
-    ux_me = rows(mine, x, r_x)
-    add_all(ux_me, ux, "x")
-    w_uy = stage("uy", "y", lambda i: rows(ux_me, i, r_y), lambda j: uy)
-    w_py()
-    pb[c, y] += py[...]
-    w_pz = stage("pz", "z", lambda i: pb.at[c, y, i], lambda j: pz.at[j])
-    w_uy()
-    uy_me = rows(ux_me, y, r_y)
-    uy_me[...] += uy[...]
-    w_uz = stage("uz", "z", lambda i: rows(uy_me, i, r_z), lambda j: uz.at[j])
-    w_uz()
-    def out_c(i):
-        return rows(unit, i, half)
-
-    def out_x(i):
-        return rows(out_c(c), i, r_x)
-
-    def out_y(i):
-        return rows(out_x(x), i, r_y)
-
-    def out_z(i):
-        return rows(out_y(y), i, r_z)
-
-    value = rows(uy_me, z, r_z)[...]
-    for k in range(1, nz):
-        value = value + uz[peer_of(z, k, nz)]
-    out_z(z)[...] = value
-    g_uz = stage("gz", "z", lambda i: out_z(z), lambda j: out_z(j))
-    g_uz()
-    g_uy = stage("gy", "y", lambda i: out_y(y), lambda j: out_y(j))
-    w_pz()
-    pz_me = pb.at[c, y, z]
-    add_all(pz_me, pz, "z")
-    w_px = stage("px", "x", lambda i: rows(pz_me, i, hx), lambda j: px.at[j])
-    g_uy()
-    g_ux = stage("gx", "x", lambda i: out_x(x), lambda j: out_x(j))
-    w_px()
-
-    def pout_c(i):
-        return rows(pout, i, hb)
-
-    def pout_x(i):
-        return rows(pout_c(c), i, hx)
-
-    value = rows(pz_me, x, hx)[...]
-    for k in range(1, nx):
-        value = value + px[peer_of(x, k, nx)]
-    pout_x(x)[...] = value
-    g_px = stage("hx", "x", lambda i: pout_x(x), lambda j: pout_x(j))
-    g_ux()
-    g_uc = stage("gc", "c", lambda i: out_c(c), lambda j: out_c(j))
-    g_px()
-    g_pc = stage("hc", "c", lambda i: pout_c(c), lambda j: pout_c(j))
-    g_uc()
-    g_pc()
+    share = block // len(PROJ_ORDERS)
+    cell = share // n_dp
+    for g in range(n_group):
+        part = dot(feat[:, g * block:(g + 1) * block], gh[...], 0, 0)
+        for s, order in enumerate(PROJ_ORDERS):
+            for i in range(n_dp):
+                spot = {"c": i // nx, "x": i % nx, "y": g % 2, "z": g // 2}
+                row = 0
+                for axis in order:
+                    row = row * axes[axis][2] + spot[axis]
+                row = s * share * n_group + row * cell
+                pb[row:row + cell] = part[s * share + i * cell:s * share + (i + 1) * cell]
+    for s, order in enumerate(PROJ_ORDERS):
+        size = share * n_group
+        own = s * share + (c * nx + x) * cell
+        stream = scatter(order, pb, s * size, size, pout, own, "xc")
+        next(stream)
+        streams.append(stream)
+
+    turn = 0
+    while streams:
+        streams = [stream for stream in streams if next(stream, 0) is None]
+        if turn == 0:
+            gfeat[...] = dot(gh[...], proj[...], 1, 1).astype(BF16)
+        turn += 1
     for copy in sends:
         copy.wait_send()
 
 
 def sums(n_dp, n_group, grad_scores, embed_b, features, grad_hidden, proj_weight):
-    nx, nz = n_dp // 2, n_group // 2
     count, feats, width = grad_scores.shape[1], features.shape[1], embed_b.shape[1]
-    half = count // 2
-    r_x = half // nx
-    r_y = r_x // 2
-    r_z = r_y // nz
-    hb = feats // n_group // 2
-    hx = hb // nx
     vmem = pl.BlockSpec(memory_space=pltpu.VMEM)
-    n_sem = 16 * max(2, nx, nz)
+    n_sem = (len(UNIT_ORDERS) + len(PROJ_ORDERS)) * 2 * (4 + n_dp // 2 + n_group // 2)
     return pl.pallas_call(
         functools.partial(sums_kernel, n_dp, n_group),
         out_shape=(
@@ -310,16 +273,9 @@
         in_specs=[vmem] * 5,
         out_specs=(vmem,) * 3,
         scratch_shapes=[
-            pltpu.VMEM((2, half, width), F32),
-            pltpu.VMEM((half, width), F32),
-            pltpu.VMEM((nx, r_x, width), F32),
-            pltpu.VMEM((r_y, width), F32),
-            pltpu.VMEM((nz, r_z, width), F32),
-            pltpu.VMEM((2, 2, nz, hb, width), F32),
-            pltpu.VMEM((2, nz, hb, width), F32),
-            pltpu.VMEM((nz, hb, width), F32),
-            pltpu.VMEM((nz, hb, width), F32),
-            pltpu.VMEM((nx, hx, width), F32),
+            pltpu.VMEM((count, width), F32),
+            pltpu.VMEM((feats, width), F32),
+            pltpu.VMEM((2 * (count + feats), width), F32),
             pltpu.SemaphoreType.DMA((n_sem,)),
             pltpu.SemaphoreType.DMA((n_sem,)),
         ],
@@ -344,7 +300,7 @@
         grad_scores, embed_b, grad_hidden = scores(
             n_dp, n_group, features, target_embed, proj_weight, prototypes)
         args = (grad_scores, embed_b, features, grad_hidden, proj_weight)
-        unit = 8 * n_dp * n_group
+        unit = 8 * n_dp * n_group * max(len(UNIT_ORDERS), len(PROJ_ORDERS))
         even = n_dp % 2 == 0 and n_group % 2 == 0
         if even and prototypes.shape[0] % unit == 0 and features.shape[1] % unit == 0:
             grad_unit, grad_proj, grad_feat = sums(n_dp, n_group, *args)

time: 123 us -> 103 us (0.84)
  Pallas kernels: 113 us -> 92.4 us
    pallas_call x1, Pallas kernels: 81.8 us -> 61.6 us  [sums(): pl.pallas_call(functools.partial(sums_kernel, n_dp, n_group), out_shape=(...]
where the time goes in v2:
time: 103 us
  Pallas kernels  92.4 us (90%)
  other arithmetic  6.12 us (6%)
  local copies, waits for them, and re-layouts  3.31 us (3%)
    pallas_call x1, Pallas kernels, sums(): pl.pallas_call(functools.partial(sums_kernel, n_dp, n_group), out_shape=(...  61.6 us
    pallas_call x1, Pallas kernels, scores(): pl.pallas_call(functools.partial(scores_kernel, n_dp, n_group), out_shape...  30.8 us
    unnamed x12, local copies, waits for them, and re-layouts  3.31 us
    reduce_sum x1, other arithmetic, local(): along = jnp.sum(unit_protos * grad_unit, axis=-1, keepdims=True)  2.37 us

profile of v2, /device:TPU:0, one launch (start us, length us, event | category | flops | bytes accessed | tf_op | source)
XLA Modules:
  0.0 102.6 jit_solution(957013347243256661)
XLA Ops:
  0.6 0.0 copy-start
  0.6 0.0 copy-start.2
  0.6 2.1 %multiply_reduce_fusion.1 = f32[2048]{0:T(1024)S(1)} fusion(f32[2048,256]{1,0:T(8,128)} %protos.1), kind=kLoop, calls=%fused_computation.2 | loop fusion | flops 1046528 | bytes 2105344 | tf_op jit(solution)/shard_map/reduce_sum | solution.py:21
  2.7 0.0 copy-done
  2.7 0.0 copy-done.2
  2.7 0.0 copy-start.1
  2.8 1.4 %copy-done.1 = bf16[3072,256]{1,0:T(8,128)(2,1)S(1)} copy-done((bf16[3072,256]{1,0:T(8,128)(2,1)S(1)}, bf16[3072,256]{1,0:T(8,128)(2,1)}, u32[]{:S(2)}) %copy-start.1) | copy-done | bytes 1572888
  4.2 30.8 %scores.1 = (bf16[256,2048]{1,0:T(8,128)(2,1)S(1)}, bf16[256,256]{1,0:T(8,128)(2,1)S(1)}, bf16[256,256]{1,0:T(8,128)(2,1)S(1)}) custom-call(bf16[256,3072]{1,0:T(8,128)(2,1)S(1)} %copy-done, bf16[256,256]{1,0:T(8,128)(2,1)S(1)} %copy-done.2, bf16[3072,256]{1,0:T(8,128)(2,1)S(1)} %copy-done.1, f32[2048,256]{1,0:T(8,128)} %protos.1), custom_call_target="tpu_custom_call" | custom-call | tf_op jit(solution)/shard_map/scores/pallas_call | solution.py:102
  35.0 0.0 copy-start.3
  35.0 61.6 %sums.1 = (f32[2048,256]{1,0:T(8,128)}, f32[384,256]{1,0:T(8,128)S(1)}, bf16[256,3072]{1,0:T(8,128)(2,1)S(1)}) custom-call(bf16[256,2048]{1,0:T(8,128)(2,1)S(1)} %get-tuple-element.9.gs, bf16[256,256]{1,0:T(8,128)(2,1)S(1)} %get-tuple-element.10.embed, bf16[256,3072]{1,0:T(8,128)(2,1)S(1)} %copy-done, bf16[256,256]{1,0:T(8,128)(2,1)S(1)} %get-tuple-element.11.gh, ...), custom_call_target="tpu_custom_call" | custom-call | tf_op jit(solution)/shard_map/sums/pallas_call | solution.py:266
  96.6 0.0 copy-done.3
  96.6 0.0 copy-start.4
  96.6 2.4 %multiply_reduce_fusion = f32[2048]{0:T(1024)S(1)} fusion(f32[2048,256]{1,0:T(8,128)} %get-tuple-element.14, f32[2048,256]{1,0:T(8,128)S(1)} %copy-done.3, f32[2048]{0:T(1024)S(1)} %add_rsqrt_fusion), kind=kLoop, calls=%fused_computation.1 | loop fusion | flops 1570816 | bytes 4210688 | tf_op jit(solution)/shard_map/reduce_sum | solution.py:311
  99.0 0.0 copy-done.4
  99.0 1.7 %subtract_multiply_fusion = f32[2048,256]{1,0:T(8,128)} fusion(f32[2048,256]{1,0:T(8,128)S(1)} %copy-done.4, f32[2048,256]{1,0:T(8,128)S(1)} %copy-done.3, f32[2048]{0:T(1024)S(1)} %multiply_reduce_fusion, f32[2048]{0:T(1024)S(1)} %add_rsqrt_fusion), kind=kLoop, calls=%fused_computation | loop fusion | flops 2097152 | bytes 6307840 | tf_op jit(solution)/shard_map/mul | solution.py:312
  100.7 1.1 %copy.9 = bf16[256,3072]{1,0:T(8,128)(2,1)} copy(bf16[256,3072]{1,0:T(8,128)(2,1)S(1)} %get-tuple-element.18) | data formatting | bytes 3145728
  101.8 0.7 copy.10
  (1 shorter events, 0.0 us)
Async XLA Ops:
  0.6 2.1 %copy-start = (bf16[256,3072]{1,0:T(8,128)(2,1)S(1)}, bf16[256,3072]{1,0:T(8,128)(2,1)}, u32[]{:S(2)}) copy-start(bf16[256,3072]{1,0:T(8,128)(2,1)} %feat.3) | copy-start | bytes 4718596
  0.6 2.1 %copy-start.2 = (bf16[256,256]{1,0:T(8,128)(2,1)S(1)}, bf16[256,256]{1,0:T(8,128)(2,1)}, u32[]{:S(2)}) copy-start(bf16[256,256]{1,0:T(8,128)(2,1)} %target.1) | copy-start | bytes 393220
  2.7 1.4 %copy-start.1 = (bf16[3072,256]{1,0:T(8,128)(2,1)S(1)}, bf16[3072,256]{1,0:T(8,128)(2,1)}, u32[]{:S(2)}) copy-start(bf16[3072,256]{1,0:T(8,128)(2,1)} %proj.3) | copy-start | bytes 4718596
  35.0 61.6 %copy-start.3 = (f32[2048,256]{1,0:T(8,128)S(1)}, f32[2048,256]{1,0:T(8,128)}, u32[]{:S(2)}) copy-start(f32[2048,256]{1,0:T(8,128)} %protos.1) | copy-start | bytes 6291460
  96.6 2.4 %copy-start.4 = (f32[2048,256]{1,0:T(8,128)S(1)}, f32[2048,256]{1,0:T(8,128)}, u32[]{:S(2)}) copy-start(f32[2048,256]{1,0:T(8,128)} %get-tuple-element.14) | copy-start | bytes 6291460

commit v3 on v2

--- a/solution.py
+++ b/solution.py
@@ -126,24 +126,31 @@
     )(features, target_embed, proj_weight, prototypes)
 
 
-UNIT_ORDERS = ("cxyz", "cyxz", "cxyz", "cyxz")
-PROJ_ORDERS = ("cyzx", "cxzy", "cyzx", "cxzy")
+UNIT_ORDERS = ("cwvxy", "cwyxv", "cxwyv", "cywvx")
+PROJ_ORDERS = ("cxwyv", "cxywv", "cywxv", "cywxv")
+GFEAT_TURN = 7
+TURNS = (
+    0, 1, 2, 3, 4, 5, 6, 7, 0, 1, 2, 3, 0, 2, 3, 1, 4, 5, 0, 3, 1, 2, 6, 7, 3, 0, 1, 4, 3, 2, 0, 1, 5, 4,
+    2, 0, 1, 3, 2, 4, 6, 7, 5, 1, 4, 3, 4, 0, 5, 6, 7, 2, 5, 5, 6, 7, 3, 1, 2, 3, 0, 6, 7, 1, 2, 6, 7, 0,
+)
 
 
 def sums_kernel(
-    n_dp, n_group, gs, embed, feat, gh, proj, unit, pout, gfeat,
-    ub, pb, landing, sem_s, sem_r,
+    n_dp, n_group, gs, embed, feat, gh, proj, protos, gprotos, pout, gfeat,
+    unit, ub, pb, landing, sem_s, sem_r,
 ):
-    nx, nz = n_dp // 2, n_group // 2
+    nx, nv = n_dp // 2, n_group // 4
     dp = lax.axis_index("dp")
     grp = lax.axis_index("group")
     x, c = dp // 2, lax.rem(dp, 2)
     z, y = grp // 2, lax.rem(grp, 2)
+    v, w = z // 2, lax.rem(z, 2)
     axes = {
         "c": (lambda i: (x * 2 + i, grp), c, 2),
         "x": (lambda i: (i * 2 + c, grp), x, nx),
         "y": (lambda i: (dp, z * 2 + i), y, 2),
-        "z": (lambda i: (dp, i * 2 + y), z, nz),
+        "w": (lambda i: (dp, (v * 2 + i) * 2 + y), w, 2),
+        "v": (lambda i: (dp, (i * 2 + w) * 2 + y), v, nv),
     }
     barrier = pltpu.get_barrier_semaphore()
     total = 0
@@ -214,18 +221,29 @@
             wait()
             base, size = low, size * n
 
-    where = {"c": c, "x": x, "y": y, "z": z}
+    where = {"c": c, "x": x, "y": y, "w": w, "v": v}
     count, feats = gs.shape[1], feat.shape[1]
     streams = []
     size = count // len(UNIT_ORDERS)
     ub[...] = dot(gs[...], embed[...], 0, 0)
     pl.semaphore_wait(barrier, total)
+
+    def finish(stream, low):
+        yield from stream
+        rows = pl.ds(low, size)
+        value = protos[rows, :]
+        scale = inv_norm(value)
+        value = value * scale
+        along = jnp.sum(value * unit[rows, :], axis=-1, keepdims=True)
+        gprotos[rows, :] = (unit[rows, :] - value * along) * scale
+
     for s, order in enumerate(UNIT_ORDERS):
         own, part = s * size, size
         for axis in order:
             part //= axes[axis][2]
             own = own + where[axis] * part
-        streams.append(scatter(order, ub, s * size, size, unit, own, order[::-1]))
+        streams.append(finish(
+            scatter(order, ub, s * size, size, unit, own, order[::-1]), s * size))
     for stream in streams:
         next(stream)
 
@@ -236,33 +254,31 @@
         part = dot(feat[:, g * block:(g + 1) * block], gh[...], 0, 0)
         for s, order in enumerate(PROJ_ORDERS):
             for i in range(n_dp):
-                spot = {"c": i // nx, "x": i % nx, "y": g % 2, "z": g // 2}
+                spot = {"c": i // nx, "x": i % nx, "y": g % 2, "w": g // 2 % 2, "v": g // 4}
                 row = 0
                 for axis in order:
                     row = row * axes[axis][2] + spot[axis]
                 row = s * share * n_group + row * cell
                 pb[row:row + cell] = part[s * share + i * cell:s * share + (i + 1) * cell]
     for s, order in enumerate(PROJ_ORDERS):
-        size = share * n_group
+        held = share * n_group
         own = s * share + (c * nx + x) * cell
-        stream = scatter(order, pb, s * size, size, pout, own, "xc")
+        stream = scatter(order, pb, s * held, held, pout, own, "xc")
         next(stream)
         streams.append(stream)
 
-    turn = 0
-    while streams:
-        streams = [stream for stream in streams if next(stream, 0) is None]
-        if turn == 0:
+    for turn, s in enumerate(TURNS):
+        next(streams[s], 0)
+        if turn == GFEAT_TURN:
             gfeat[...] = dot(gh[...], proj[...], 1, 1).astype(BF16)
-        turn += 1
     for copy in sends:
         copy.wait_send()
 
 
-def sums(n_dp, n_group, grad_scores, embed_b, features, grad_hidden, proj_weight):
+def sums(n_dp, n_group, grad_scores, embed_b, features, grad_hidden, proj_weight, prototypes):
     count, feats, width = grad_scores.shape[1], features.shape[1], embed_b.shape[1]
     vmem = pl.BlockSpec(memory_space=pltpu.VMEM)
-    n_sem = (len(UNIT_ORDERS) + len(PROJ_ORDERS)) * 2 * (4 + n_dp // 2 + n_group // 2)
+    n_sem = (len(UNIT_ORDERS) + len(PROJ_ORDERS)) * 2 * (6 + n_dp // 2 + n_group // 4)
     return pl.pallas_call(
         functools.partial(sums_kernel, n_dp, n_group),
         out_shape=(
@@ -270,9 +286,10 @@
             jax.ShapeDtypeStruct((feats // n_group, width), F32),
             jax.ShapeDtypeStruct(features.shape, BF16),
         ),
-        in_specs=[vmem] * 5,
+        in_specs=[vmem] * 6,
         out_specs=(vmem,) * 3,
         scratch_shapes=[
+            pltpu.VMEM((count, width), F32),
             pltpu.VMEM((count, width), F32),
             pltpu.VMEM((feats, width), F32),
             pltpu.VMEM((2 * (count + feats), width), F32),
@@ -282,7 +299,7 @@
         compiler_params=pltpu.CompilerParams(
             collective_id=1, has_side_effects=True, vmem_limit_bytes=48 << 20),
         name="sums",
-    )(grad_scores, embed_b, features, grad_hidden, proj_weight)
+    )(grad_scores, embed_b, features, grad_hidden, proj_weight, prototypes)
 
 
 def plain_sums(grad_scores, embed_b, features, grad_hidden, proj_weight):
@@ -301,11 +318,11 @@
             n_dp, n_group, features, target_embed, proj_weight, prototypes)
         args = (grad_scores, embed_b, features, grad_hidden, proj_weight)
         unit = 8 * n_dp * n_group * max(len(UNIT_ORDERS), len(PROJ_ORDERS))
-        even = n_dp % 2 == 0 and n_group % 2 == 0
+        even = n_dp % 2 == 0 and n_group % 4 == 0
         if even and prototypes.shape[0] % unit == 0 and features.shape[1] % unit == 0:
-            grad_unit, grad_proj, grad_feat = sums(n_dp, n_group, *args)
-        else:
-            grad_unit, grad_proj, grad_feat = plain_sums(*args)
+            grad_protos, grad_proj, grad_feat = sums(n_dp, n_group, *args, prototypes)
+            return (grad_feat, grad_proj, grad_protos)
+        grad_unit, grad_proj, grad_feat = plain_sums(*args)
         scale = inv_norm(prototypes)
         unit_protos = prototypes * scale
         along = jnp.sum(unit_protos * grad_unit, axis=-1, keepdims=True)

time: 103 us -> 91.6 us (0.89)
  Pallas kernels: 92.4 us -> 83.2 us
  other arithmetic: 6.12 us -> 0 us
  local copies, waits for them, and re-layouts: 3.31 us -> 7.25 us
    pallas_call x1, Pallas kernels: 61.6 us -> 52.4 us  [sums(): pl.pallas_call(functools.partial(sums_kernel, n_dp, n_group), out_shape=(...]
    reduce_sum x2 -> x0, other arithmetic: 4.43 us -> none  [the longest x1 2.37 us: local(): along = jnp.sum(unit_protos * grad_unit, axis=-1, keepdims=True)]
    unnamed x12 -> x11, local copies, waits for them, and re-layouts: 3.31 us -> 7.25 us
    mul x1 -> x0, other arithmetic: 1.69 us -> none  [local(): grad_protos = (grad_unit - unit_protos * along) * scale]
where the time goes in v3:
time: 91.6 us; the launch traced here: 91.1 us
  Pallas kernels  83.2 us (91%)
  local copies, waits for them, and re-layouts  7.25 us (8%)
    pallas_call x1, Pallas kernels, sums(): pl.pallas_call(functools.partial(sums_kernel, n_dp, n_group), out_shape=(...  52.4 us
    pallas_call x1, Pallas kernels, scores(): pl.pallas_call(functools.partial(scores_kernel, n_dp, n_group), out_shape...  30.8 us
    unnamed x11, local copies, waits for them, and re-layouts  7.25 us

profile of v3, /device:TPU:0, one launch (start us, length us, event | category | flops | bytes accessed | tf_op | source)
XLA Modules:
  0.0 91.1 jit_solution(16922179752735692231)
XLA Ops:
  0.6 0.0 copy-start
  0.6 1.4 %copy-done = bf16[256,3072]{1,0:T(8,128)(2,1)S(1)} copy-done((bf16[256,3072]{1,0:T(8,128)(2,1)S(1)}, bf16[256,3072]{1,0:T(8,128)(2,1)}, u32[]{:S(2)}) %copy-start) | copy-done | bytes 1572888
  2.0 0.0 copy-start.1
  2.0 1.4 %copy-done.1 = bf16[3072,256]{1,0:T(8,128)(2,1)S(1)} copy-done((bf16[3072,256]{1,0:T(8,128)(2,1)S(1)}, bf16[3072,256]{1,0:T(8,128)(2,1)}, u32[]{:S(2)}) %copy-start.1) | copy-done | bytes 1572888
  3.4 0.0 copy-start.2
  3.4 0.9 copy-done.2
  4.4 30.8 %scores.1 = (bf16[256,2048]{1,0:T(8,128)(2,1)S(1)}, bf16[256,256]{1,0:T(8,128)(2,1)S(1)}, bf16[256,256]{1,0:T(8,128)(2,1)S(1)}) custom-call(bf16[256,3072]{1,0:T(8,128)(2,1)S(1)} %copy-done, bf16[256,256]{1,0:T(8,128)(2,1)S(1)} %copy-done.2, bf16[3072,256]{1,0:T(8,128)(2,1)S(1)} %copy-done.1, f32[2048,256]{1,0:T(8,128)} %protos.3), custom_call_target="tpu_custom_call" | custom-call | tf_op jit(solution)/shard_map/scores/pallas_call | solution.py:102
  35.2 52.4 %sums.1 = (f32[2048,256]{1,0:T(8,128)}, f32[384,256]{1,0:T(8,128)S(1)}, bf16[256,3072]{1,0:T(8,128)(2,1)S(1)}) custom-call(bf16[256,2048]{1,0:T(8,128)(2,1)S(1)} %get-tuple-element.9.gs, bf16[256,256]{1,0:T(8,128)(2,1)S(1)} %get-tuple-element.10.embed, bf16[256,3072]{1,0:T(8,128)(2,1)S(1)} %copy-done, bf16[256,256]{1,0:T(8,128)(2,1)S(1)} %get-tuple-element.11.gh, ...), custom_call_target="tpu_custom_call" | custom-call | tf_op jit(solution)/shard_map/sums/pallas_call | solution.py:282
  87.6 0.0 copy-start.3
  87.6 1.1 %copy.10 = bf16[256,3072]{1,0:T(8,128)(2,1)} copy(bf16[256,3072]{1,0:T(8,128)(2,1)S(1)} %get-tuple-element.18) | data formatting | bytes 3145728
  88.7 0.7 copy.11
  89.5 0.3 copy-done.3
  89.8 1.3 %copy.12 = f32[2048,256]{1,0:T(8,128)} copy(f32[2048,256]{1,0:T(8,128)S(1)} %copy-done.3) | data formatting | bytes 4194304
Async XLA Ops:
  0.6 1.4 %copy-start = (bf16[256,3072]{1,0:T(8,128)(2,1)S(1)}, bf16[256,3072]{1,0:T(8,128)(2,1)}, u32[]{:S(2)}) copy-start(bf16[256,3072]{1,0:T(8,128)(2,1)} %feat.3) | copy-start | bytes 4718596
  2.0 1.4 %copy-start.1 = (bf16[3072,256]{1,0:T(8,128)(2,1)S(1)}, bf16[3072,256]{1,0:T(8,128)(2,1)}, u32[]{:S(2)}) copy-start(bf16[3072,256]{1,0:T(8,128)(2,1)} %proj.3) | copy-start | bytes 4718596
  3.4 0.9 copy-start.2
  87.6 2.2 %copy-start.3 = (f32[2048,256]{1,0:T(8,128)S(1)}, f32[2048,256]{1,0:T(8,128)}, u32[]{:S(2)}) copy-start(f32[2048,256]{1,0:T(8,128)} %get-tuple-element.20) | copy-start | bytes 6291460
